TPU v7x, 256 devices: a whole 4x4x8 slice. The times are simulated.
256 devices in a mesh: tm: 32 (over x, y, core), row: 8 (over z).
Axes of the slice: x: 4, y: 4, z: 8, core: 2. Of those that a mesh axis runs over, the one named last changes fastest.
Arguments:
- frames_in: bfloat16 [64, 32, 64, 256], P('tm', 'row'), may hold values from -6 to 6
- cotangent: bfloat16 [64, 32, 64, 256], P('tm', 'row'), may hold values from -6 to 6
- kernel: bfloat16 [9, 256, 256], replicated, may hold values from -0.125 to 0.125
- readout: bfloat16 [256, 256], replicated, may hold values from -0.375 to 0.375
- feedthrough: float32 [256], replicated, may hold values from 0.5 to 1.5
- decay_rate: float32 [64, 256], P('tm'), may hold values from 0.05 to 1, as said below
- start_state: float32 [32, 64, 256], P('row'), may hold values from -6 to 6
Outputs:
- grad_frames: bfloat16 [64, 32, 64, 256], P('tm', 'row')
- grad_kernel: float32 [9, 256, 256], P(None, 'row')
- grad_readout: float32 [256, 256], P(None, 'row')
Inputs may be any that keep to these rules, and one draw needn't show every extreme that they name: `decay_rate`: every entry lies strictly between 0 and 1.
All inputs are finite; a program needn't handle non-finite values.
Results may differ from a plain program's by a relative error of at most 0.015.
Values may be sent and summed in bfloat16 or wider, within the bound.
No kernel may reach another device: no remote copies, remote signals or barrier semaphores. Data moves between devices by JAX's collectives and lax.ppermute only.
A program may use at most 64 MiB of HBM per device.

v0:
```python
import math
import jax
import jax.numpy as jnp
from jax import lax
from jax.sharding import PartitionSpec as P

SQRT_TWO_PI = 0.7978845608
CUBIC = 0.044715


def extended(cells, sides, width):
    for axis, dim in sides:
        count = lax.axis_size(axis)
        ends = count - 1
        head = lax.slice_in_dim(cells, 0, width, axis=dim)
        tail = lax.slice_in_dim(cells, cells.shape[dim] - width, cells.shape[dim], axis=dim)
        cells = jnp.concatenate(
            [
                lax.ppermute(tail, axis, [(i, (i + 1) % count) for i in range(ends)]),
                cells,
                lax.ppermute(head, axis, [((i + 1) % count, i) for i in range(ends)]),
            ],
            axis=dim,
        )
    return cells


def carried_in(value, axis, join, neutral, backward):
    count, mine = (lax.axis_size(axis), lax.axis_index(axis))
    pieces = jax.tree.map(lambda part: lax.all_gather(part, axis), value)
    if backward:
        pieces = jax.tree.map(lambda part: part[::-1], pieces)
        mine = count - 1 - mine
    subtotal = jax.tree.map(
        lambda part, zero: jnp.full_like(part, 0) + jnp.asarray(zero, part.dtype), value, neutral
    )

    def turn(position, subtotal):
        longer = join(subtotal, jax.tree.map(lambda part: part[position], pieces))
        return jax.tree.map(lambda new, old: jnp.where(position < mine, new, old), longer, subtotal)

    return lax.fori_loop(0, count - 1, turn, subtotal)


def gelu_slope(mixture):
    inside = SQRT_TWO_PI * (mixture + CUBIC * mixture * mixture * mixture)
    tangent = jnp.tanh(inside)
    return 0.5 * (1.0 + tangent) + 0.5 * mixture * (1.0 - tangent * tangent) * SQRT_TWO_PI * (
        1.0 + 3.0 * CUBIC * mixture * mixture
    )


def block_taps(padded, band_rows, grid_width, flipped):
    pieces = []
    for vertical in range(3):
        for lateral in range(3):
            from_top = 2 - vertical if flipped else vertical
            from_left = 2 - lateral if flipped else lateral
            pieces.append(
                padded[:, from_top : from_top + band_rows, from_left : from_left + grid_width, :]
            )
    return jnp.stack(pieces, axis=3)


def compose(earlier, later):
    return (later[0] * earlier[0], later[0] * earlier[1] + later[1])


def local(frames_in, cotangent, kernel, readout, feedthrough, decay_rate, start_state):
    frames_here, band_rows, grid_width, channels = frames_in.shape
    state_width = kernel.shape[2]
    cell_count = frames_here * band_rows * grid_width
    rimmed = extended(frames_in, (("row", 1),), 1)
    padded = jnp.pad(rimmed, ((0, 0), (0, 0), (1, 1), (0, 0)))
    input_taps = block_taps(padded, band_rows, grid_width, False).reshape(cell_count, 9 * channels)
    driven = jnp.dot(
        input_taps, kernel.reshape(9 * channels, state_width), preferred_element_type=jnp.float32
    )
    driven = driven.reshape(frames_here, band_rows, grid_width, state_width)
    gain_all = jnp.sqrt(1.0 - decay_rate * decay_rate)
    leader = (lax.axis_index("tm") == 0).astype(jnp.float32)

    def advance(carried, inputs):
        driven_now, rate_now, gain_now = inputs
        carried = rate_now * carried + gain_now * driven_now
        return (carried, carried)

    _, local_states = lax.scan(advance, start_state * leader, (driven, decay_rate, gain_all))
    through = jnp.cumprod(decay_rate, axis=0)
    identity = (
        jnp.ones((state_width,), jnp.float32),
        jnp.zeros((band_rows, grid_width, state_width), jnp.float32),
    )
    _, entering = carried_in((through[-1], local_states[-1]), "tm", compose, identity, False)
    states = local_states + through[:, None, None, :] * entering[None]
    state_bf = states.astype(jnp.bfloat16).reshape(cell_count, state_width)
    mixture = jnp.dot(state_bf, readout, preferred_element_type=jnp.float32)
    slope_bf = (
        cotangent.reshape(cell_count, channels).astype(jnp.float32) * gelu_slope(mixture)
    ).astype(jnp.bfloat16)
    pulled = lax.dot_general(
        slope_bf, readout, (((1,), (1,)), ((), ())), preferred_element_type=jnp.float32
    )
    pulled = pulled.reshape(frames_here, band_rows, grid_width, state_width)
    later_rate = jnp.concatenate([decay_rate[1:], jnp.ones((1, state_width), jnp.float32)], axis=0)

    def retreat(carried, inputs):
        pulled_now, rate_next = inputs
        carried = pulled_now + rate_next * carried
        return (carried, carried)

    _, local_adjoint = lax.scan(
        retreat,
        jnp.zeros((band_rows, grid_width, state_width), jnp.float32),
        (pulled, later_rate),
        reverse=True,
    )
    remaining = jnp.flip(jnp.cumprod(jnp.flip(later_rate, 0), axis=0), 0)
    _, arriving = carried_in(
        (through[-1], decay_rate[0][None, None, :] * local_adjoint[0]),
        "tm",
        compose,
        identity,
        True,
    )
    adjoint = local_adjoint + remaining[:, None, None, :] * arriving[None]
    grad_drive = (gain_all[:, None, None, :] * adjoint).astype(jnp.bfloat16)
    rim_adjoint = extended(grad_drive, (("row", 1),), 1)
    padded_drive = jnp.pad(rim_adjoint, ((0, 0), (0, 0), (1, 1), (0, 0)))
    output_taps = block_taps(padded_drive, band_rows, grid_width, True).reshape(
        cell_count, 9, state_width
    )
    spread = lax.dot_general(
        output_taps, kernel, (((1, 2), (0, 2)), ((), ())), preferred_element_type=jnp.float32
    )
    spread = spread.reshape(frames_here, band_rows, grid_width, channels)
    grad_frames = (spread + feedthrough * cotangent.astype(jnp.float32)).astype(jnp.bfloat16)
    kernel_term = lax.dot_general(
        input_taps,
        grad_drive.reshape(cell_count, state_width),
        (((0,), (0,)), ((), ())),
        preferred_element_type=jnp.float32,
    ).reshape(9, channels, state_width)
    readout_term = lax.dot_general(
        state_bf, slope_bf, (((0,), (0,)), ((), ())), preferred_element_type=jnp.float32
    )
    band_count = lax.axis_size("row")
    scaling = 1.0 / math.sqrt(cell_count * lax.axis_size("tm") * band_count)
    share_width = channels // band_count
    kernel_all, readout_all = lax.psum((kernel_term, readout_term), ("tm", "row"))
    offset_start = lax.axis_index("row") * share_width
    kernel_part = lax.dynamic_slice_in_dim(kernel_all, offset_start, share_width, 1)
    readout_part = lax.dynamic_slice_in_dim(readout_all, offset_start, share_width, 1)
    return (grad_frames, kernel_part * scaling, readout_part * scaling)


def solution(mesh):
    placed = (
        P("tm", "row", None, None),
        P("tm", "row", None, None),
        P(),
        P(),
        P(),
        P("tm", None),
        P("row", None, None),
    )
    return jax.shard_map(
        local,
        mesh=mesh,
        in_specs=placed,
        out_specs=(P("tm", "row", None, None), P(None, "row", None), P(None, "row")),
        check_vma=False,
    )
```

profile of v0, /device:TPU:2, one launch (start us, length us, event | category | flops | bytes accessed | tf_op | source)
XLA Modules:
  0.0 510.4 jit_solution(2149309793703916554)
XLA Ops:
  8.2 3.8 collective-permute-start
  12.1 1.3 collective-permute-start.1
  15.1 3.2 collective-permute-done.1
  23.3 24.2 %all-gather = f32[32,1,256]{2,1,0:T(1,128)S(1)} all-gather(f32[1,1,256]{2,1,0:T(1,128)S(1)} %slice_bitcast_fusion.12), channel_id=1, replica_groups=mesh['tm'=32,'row'=8] {'tm'}, dimensions={0}, use_global_device_ids=true | all-gather | bytes 33792 | tf_op jit(solution)/shard_map/all_gather | solution.py:30
  47.6 36.4 %all-gather.4.cloned.1.call-done = f32[32,4,64,256]{3,2,1,0:T(8,128)} async-done(((f32[1,4,64,256]{3,2,1,0:T(8,128)}), f32[32,4,64,256]{3,2,1,0:T(8,128)}) %all-gather.4.cloned.1.call-update) | async-done | bytes 8388624 | tf_op jit(solution)/shard_map/all_gather | solution.py:30
  84.0 36.9 %while.58 = (s32[]{:T(128)}, f32[4,64,256]{2,1,0:T(8,128)S(1)}, s32[]{:T(128)}, f32[32,256]{1,0:T(8,128)S(1)}, f32[32,4,64,256]{3,2,1,0:T(8,128)}, /*index=5*/s32[]{:T(128)}, s32[]{:T(128)}) while((s32[]{:T(128)}, f32[4,64,256]{2,1,0:T(8,128)S(1)}, s32[]{:T(128)}, f32[32,256]{1,0:T(8,128)S(1)}, f32[32,4,64,256]{3,2,1,0:T(8,128)}, ...), condition=%wide.region_4.5_spmd.clone, body=%wide.region_3.4_spmd.clone.sunk | while | flops 262148 | bytes 789609 | solution.py:42
  84.0 1.2 fusion.59
  85.2 1.1 fusion.59
  86.4 1.1 fusion.59
  87.6 1.1 fusion.59
  88.8 1.1 fusion.59
  90.0 1.1 fusion.59
  91.2 1.1 fusion.59
  92.4 1.1 fusion.59
  93.5 1.1 fusion.59
  94.7 1.1 fusion.59
  95.9 1.1 fusion.59
  97.1 1.1 fusion.59
  98.3 1.1 fusion.59
  99.5 1.1 fusion.59
  100.7 1.1 fusion.59
  101.9 1.1 fusion.59
  103.1 1.1 fusion.59
  104.3 1.1 fusion.59
  105.4 1.1 fusion.59
  106.6 1.1 fusion.59
  107.8 1.1 fusion.59
  109.0 1.1 fusion.59
  110.2 1.1 fusion.59
  111.4 1.1 fusion.59
  112.6 1.1 fusion.59
  113.8 1.1 fusion.59
  115.0 1.1 fusion.59
  116.1 1.1 fusion.59
  117.3 1.1 fusion.59
  118.5 1.1 fusion.59
  119.7 1.1 fusion.59
  123.2 3.3 copy.51
  126.5 2.8 copy.57
  129.3 4.3 copy.52
  134.5 45.9 %all-gather.6.cloned.1.call-done = f32[32,4,64,256]{3,2,1,0:T(8,128)} async-done(((f32[1,4,64,256]{3,2,1,0:T(8,128)}), f32[32,4,64,256]{3,2,1,0:T(8,128)}) %all-gather.6.cloned.1.call-update) | async-done | bytes 8388624 | tf_op jit(solution)/shard_map/all_gather | solution.py:30
  180.4 7.7 %rev.16 = f32[32,4,64,256]{3,2,1,0:T(8,128)} reverse(f32[32,4,64,256]{3,2,1,0:T(8,128)} %all-gather.6.cloned.1.call-done), dimensions={0} | reverse | bytes 16777216 | tf_op jit(solution)/shard_map/rev | solution.py:32
  188.1 36.8 %while.60 = (s32[]{:T(128)}, f32[4,64,256]{2,1,0:T(8,128)S(1)}, s32[]{:T(128)}, f32[32,256]{1,0:T(8,128)S(1)}, f32[32,4,64,256]{3,2,1,0:T(8,128)}, /*index=5*/s32[]{:T(128)}, s32[]{:T(128)}) while((s32[]{:T(128)}, f32[4,64,256]{2,1,0:T(8,128)S(1)}, s32[]{:T(128)}, f32[32,256]{1,0:T(8,128)S(1)}, f32[32,4,64,256]{3,2,1,0:T(8,128)}, ...), condition=%wide.region_9.10_spmd.clone, body=%wide.region_8.9_spmd.clone.sunk | while | flops 262148 | bytes 789609 | solution.py:42
  189.3 1.1 fusion.60
  190.5 1.1 fusion.60
  191.7 1.1 fusion.60
  192.9 1.1 fusion.60
  194.1 1.1 fusion.60
  195.3 1.1 fusion.60
  196.5 1.1 fusion.60
  197.7 1.1 fusion.60
  198.8 1.1 fusion.60
  200.0 1.1 fusion.60
  201.2 1.1 fusion.60
  202.4 1.1 fusion.60
  203.6 1.1 fusion.60
  204.8 1.1 fusion.60
  225.1 3.5 collective-permute-start.2
  228.6 1.3 collective-permute-start.3
  229.9 3.9 fusion.45
  235.9 1.5 fusion.4
  237.4 263.4 %all-reduce.6.cloned.1.call-done = (f32[9,256,256]{2,1,0:T(8,128)}, f32[256,256]{0,1:T(8,128)}) async-done(((f32[9,256,256]{2,1,0:T(8,128)}, f32[256,256]{0,1:T(8,128)}), (f32[9,256,256]{2,1,0:T(8,128)}, f32[256,256]{0,1:T(8,128)})) %all-reduce.6.cloned.1.call-update) | async-done | bytes 2621456 | tf_op jit(solution)/shard_map/psum | solution.py:150
  500.8 1.7 dynamic-slice_multiply_fusion
  502.5 1.4 dynamic-slice_multiply_fusion.1
  (160 shorter events, 33.6 us)
Async XLA Ops:
  7.2 13.5 %copy-start = (bf16[9,256,256]{2,1,0:T(8,128)(2,1)S(1)}, bf16[9,256,256]{2,1,0:T(8,128)(2,1)}, u32[]{:S(2)}) copy-start(bf16[9,256,256]{2,1,0:T(8,128)(2,1)} %param.17) | copy-start | bytes 3538948
  7.2 13.2 %copy-start.1 = (bf16[2,4,64,256]{3,2,1,0:T(8,128)(2,1)S(1)}, bf16[2,4,64,256]{3,2,1,0:T(8,128)(2,1)}, u32[]{:S(2)}) copy-start(bf16[2,4,64,256]{3,2,1,0:T(8,128)(2,1)} %param.15) | copy-start | bytes 786436
  7.2 76.8 %all-gather.4.cloned.1.call-start = ((), (), s32[]{:S(2)}) async-start(), calls=%async_computation | async-start | bytes 8650752 | tf_op jit(solution)/shard_map/all_gather | solution.py:30
  8.2 6.8 %collective-permute-start = (bf16[2,1,64,256]{3,2,1,0:T(8,128)(2,1)S(1)}, bf16[2,1,64,256]{3,2,1,0:T(8,128)(2,1)S(1)}, u32[]{:S(2)}, u32[]{:S(2)}) collective-permute-start(bf16[2,1,64,256]{3,2,1,0:T(8,128)(2,1)S(1)} %get-tuple-element.436), channel_id=1, source_target_pairs={{0,1},{1,2},{2,3},{3,4},{4,5},{5,6},{6,7},{8,9},{9,10},{10,11},{11... | collective-permute-start | bytes 196616 | tf_op jit(solution)/shard_map/ppermute | solution.py:19
  12.1 6.2 %collective-permute-start.1 = (bf16[2,1,64,256]{3,2,1,0:T(8,128)(2,1)S(1)}, bf16[2,1,64,256]{3,2,1,0:T(8,128)(2,1)S(1)}, u32[]{:S(2)}, u32[]{:S(2)}) collective-permute-start(bf16[2,1,64,256]{3,2,1,0:T(8,128)(2,1)S(1)} %get-tuple-element.437), channel_id=1, source_target_pairs={{1,0},{2,1},{3,2},{4,3},{5,4},{6,5},{7,6},{9,8},{10,9},{11,10},{12... | collective-permute-start | bytes 196616 | tf_op jit(solution)/shard_map/ppermute | solution.py:21
  20.6 1.5 copy-start.2
  20.6 1.5 copy-start.4
  23.2 157.2 %all-gather.6.cloned.1.call-start = ((), (), s32[]{:S(2)}) async-start(), calls=%async_computation.1 | async-start | bytes 8650752 | tf_op jit(solution)/shard_map/all_gather | solution.py:30
  84.0 37.0 %copy-start.3 = (bf16[256,256]{1,0:T(8,128)(2,1)S(1)}, bf16[256,256]{1,0:T(8,128)(2,1)}, u32[]{:S(2)}) copy-start(bf16[256,256]{1,0:T(8,128)(2,1)} %param.18) | copy-start | bytes 393220
  84.0 37.0 %copy-start.5 = (bf16[2,4,64,256]{3,2,1,0:T(8,128)(2,1)S(1)}, bf16[2,4,64,256]{3,2,1,0:T(8,128)(2,1)}, u32[]{:S(2)}) copy-start(bf16[2,4,64,256]{3,2,1,0:T(8,128)(2,1)} %param.16) | copy-start | bytes 786436
  122.8 378.0 %all-reduce.6.cloned.1.call-start = ((), (), s32[]{:S(2)}) async-start(), calls=%async_computation.2 | async-start | bytes 5242880 | tf_op jit(solution)/shard_map/psum | solution.py:150
  225.1 8.7 %collective-permute-start.2 = (bf16[2,1,64,256]{3,2,1,0:T(8,128)(2,1)S(1)}, bf16[2,1,64,256]{3,2,1,0:T(8,128)(2,1)S(1)}, u32[]{:S(2)}, u32[]{:S(2)}) collective-permute-start(bf16[2,1,64,256]{3,2,1,0:T(8,128)(2,1)S(1)} %get-tuple-element.434), channel_id=1, source_target_pairs={{0,1},{1,2},{2,3},{3,4},{4,5},{5,6},{6,7},{8,9},{9,10},{10,11},{11... | collective-permute-start | bytes 196616 | tf_op jit(solution)/shard_map/ppermute | solution.py:19
  228.6 6.2 %collective-permute-start.3 = (bf16[2,1,64,256]{3,2,1,0:T(8,128)(2,1)S(1)}, bf16[2,1,64,256]{3,2,1,0:T(8,128)(2,1)S(1)}, u32[]{:S(2)}, u32[]{:S(2)}) collective-permute-start(bf16[2,1,64,256]{3,2,1,0:T(8,128)(2,1)S(1)} %get-tuple-element.435), channel_id=1, source_target_pairs={{1,0},{2,1},{3,2},{4,3},{5,4},{6,5},{7,6},{9,8},{10,9},{11,10},{12... | collective-permute-start | bytes 196616 | tf_op jit(solution)/shard_map/ppermute | solution.py:21
  234.9 1.0 copy-start.6
  234.9 0.9 copy-start.7
Sparse Core Ops, SparseCore 0:
  23.3 60.6 all-gather.3
  122.9 57.4 all-gather.5
  233.9 266.8 all-reduce.5
where the time goes:
time: 513 us; the launch traced here: 510 us
  waiting for transfers between devices  350 us (68%)
  other arithmetic  79.8 us (16%)
  blocking collectives  24.2 us (5%)
  local copies, waits for them, and re-layouts  22.5 us (4%)
  between operations  14.2 us (3%)
  starting transfers between devices  9.99 us (2%)
  matrix products  7.92 us (2%)
    psum x1, waiting for transfers between devices, local(): lax.psum((kernel_term, readout_term), ('tm', 'row'))  263 us
    all_gather x2, waiting for transfers between devices, carried_in(): pieces = jax.tree.map(lambda part: lax.all_gather(part, axis), value)  82.3 us
    select_n x62, other arithmetic, turn(): jnp.where(position < mine, new, old)  71.3 us
    all_gather x1, blocking collectives, carried_in(): pieces = jax.tree.map(lambda part: lax.all_gather(part, axis), value)  24.2 us
  transfers between devices with their start and end apart: 7, of which 5 were waited for; matrix products, arithmetic and copies ran while one was open for 4% of the time, Pallas kernels for 0%

commit v1 on v0

--- a/solution.py
+++ b/solution.py
@@ -6,6 +6,11 @@
 
 SQRT_TWO_PI = 0.7978845608
 CUBIC = 0.044715
+
+
+def one_after_other(array, one, other):
+    inner = lax.psum(array, one)
+    return lax.psum(inner, other)
 
 
 def extended(cells, sides, width):
@@ -147,7 +152,7 @@
     band_count = lax.axis_size("row")
     scaling = 1.0 / math.sqrt(cell_count * lax.axis_size("tm") * band_count)
     share_width = channels // band_count
-    kernel_all, readout_all = lax.psum((kernel_term, readout_term), ("tm", "row"))
+    kernel_all, readout_all = one_after_other((kernel_term, readout_term), "tm", "row")
     offset_start = lax.axis_index("row") * share_width
     kernel_part = lax.dynamic_slice_in_dim(kernel_all, offset_start, share_width, 1)
     readout_part = lax.dynamic_slice_in_dim(readout_all, offset_start, share_width, 1)

time: 513 us -> 448 us (0.87)
  waiting for transfers between devices: 350 us -> 284 us
    psum x1 -> x2, waiting for transfers between devices: 263 us -> 194 us  [the longest x1 118 us: one_after_other(): inner = lax.psum(array, one)]
  transfers between devices with their start and end apart: 7 -> 8, of which waited for: 5 -> 7; matrix products, arithmetic and copies ran while one was open for 4% -> 3% of each run, Pallas kernels for 0% -> 0%
where the time goes in v1:
time: 448 us; the launch traced here: 445 us
  waiting for transfers between devices  284 us (63%)
  other arithmetic  79.8 us (18%)
  blocking collectives  24.2 us (5%)
  local copies, waits for them, and re-layouts  22.6 us (5%)
  between operations  14.2 us (3%)
  starting transfers between devices  10 us (2%)
  matrix products  7.92 us (2%)
    psum x1, waiting for transfers between devices, one_after_other(): inner = lax.psum(array, one)  118 us
    all_gather x2, waiting for transfers between devices, carried_in(): pieces = jax.tree.map(lambda part: lax.all_gather(part, axis), value)  82.3 us
    psum x1, waiting for transfers between devices, one_after_other(): return lax.psum(inner, other)  76.2 us
    select_n x62, other arithmetic, turn(): jnp.where(position < mine, new, old)  71.3 us
    all_gather x1, blocking collectives, carried_in(): pieces = jax.tree.map(lambda part: lax.all_gather(part, axis), value)  24.2 us
  transfers between devices with their start and end apart: 8, of which 7 were waited for; matrix products, arithmetic and copies ran while one was open for 3% of the time, Pallas kernels for 0%

profile of v1, /device:TPU:2, one launch (start us, length us, event | category | flops | bytes accessed | tf_op | source)
XLA Modules:
  0.0 445.1 jit_solution(11240163577290987358)
XLA Ops:
  8.2 3.8 collective-permute-start
  12.1 1.3 collective-permute-start.1
  15.1 3.2 collective-permute-done.1
  23.3 24.2 %all-gather = f32[32,1,256]{2,1,0:T(1,128)S(1)} all-gather(f32[1,1,256]{2,1,0:T(1,128)S(1)} %slice_bitcast_fusion.12), channel_id=1, replica_groups=mesh['tm'=32,'row'=8] {'tm'}, dimensions={0}, use_global_device_ids=true | all-gather | bytes 33792 | tf_op jit(solution)/shard_map/all_gather | solution.py:35
  47.6 36.4 %all-gather.4.cloned.1.call-done = f32[32,4,64,256]{3,2,1,0:T(8,128)} async-done(((f32[1,4,64,256]{3,2,1,0:T(8,128)}), f32[32,4,64,256]{3,2,1,0:T(8,128)}) %all-gather.4.cloned.1.call-update) | async-done | bytes 8388624 | tf_op jit(solution)/shard_map/all_gather | solution.py:35
  84.0 36.9 %while.58 = (s32[]{:T(128)}, f32[4,64,256]{2,1,0:T(8,128)S(1)}, s32[]{:T(128)}, f32[32,256]{1,0:T(8,128)S(1)}, f32[32,4,64,256]{3,2,1,0:T(8,128)}, /*index=5*/s32[]{:T(128)}, s32[]{:T(128)}) while((s32[]{:T(128)}, f32[4,64,256]{2,1,0:T(8,128)S(1)}, s32[]{:T(128)}, f32[32,256]{1,0:T(8,128)S(1)}, f32[32,4,64,256]{3,2,1,0:T(8,128)}, ...), condition=%wide.region_4.5_spmd.clone, body=%wide.region_3.4_spmd.clone.sunk | while | flops 262148 | bytes 789609 | solution.py:47
  84.0 1.2 fusion.59
  85.2 1.1 fusion.59
  86.4 1.1 fusion.59
  87.6 1.1 fusion.59
  88.8 1.1 fusion.59
  90.0 1.1 fusion.59
  91.2 1.1 fusion.59
  92.4 1.1 fusion.59
  93.6 1.1 fusion.59
  94.7 1.1 fusion.59
  95.9 1.1 fusion.59
  97.1 1.1 fusion.59
  98.3 1.1 fusion.59
  99.5 1.1 fusion.59
  100.7 1.1 fusion.59
  101.9 1.1 fusion.59
  103.1 1.1 fusion.59
  104.3 1.1 fusion.59
  105.5 1.1 fusion.59
  106.6 1.1 fusion.59
  107.8 1.1 fusion.59
  109.0 1.1 fusion.59
  110.2 1.1 fusion.59
  111.4 1.1 fusion.59
  112.6 1.1 fusion.59
  113.8 1.1 fusion.59
  115.0 1.1 fusion.59
  116.2 1.1 fusion.59
  117.3 1.1 fusion.59
  118.5 1.1 fusion.59
  119.7 1.1 fusion.59
  123.2 3.3 copy.51
  126.5 2.8 copy.57
  129.3 4.3 copy.52
  134.6 45.9 %all-gather.6.cloned.1.call-done = f32[32,4,64,256]{3,2,1,0:T(8,128)} async-done(((f32[1,4,64,256]{3,2,1,0:T(8,128)}), f32[32,4,64,256]{3,2,1,0:T(8,128)}) %all-gather.6.cloned.1.call-update) | async-done | bytes 8388624 | tf_op jit(solution)/shard_map/all_gather | solution.py:35
  180.4 7.7 %rev.16 = f32[32,4,64,256]{3,2,1,0:T(8,128)} reverse(f32[32,4,64,256]{3,2,1,0:T(8,128)} %all-gather.6.cloned.1.call-done), dimensions={0} | reverse | bytes 16777216 | tf_op jit(solution)/shard_map/rev | solution.py:37
  188.2 36.8 %while.60 = (s32[]{:T(128)}, f32[4,64,256]{2,1,0:T(8,128)S(1)}, s32[]{:T(128)}, f32[32,256]{1,0:T(8,128)S(1)}, f32[32,4,64,256]{3,2,1,0:T(8,128)}, /*index=5*/s32[]{:T(128)}, s32[]{:T(128)}) while((s32[]{:T(128)}, f32[4,64,256]{2,1,0:T(8,128)S(1)}, s32[]{:T(128)}, f32[32,256]{1,0:T(8,128)S(1)}, f32[32,4,64,256]{3,2,1,0:T(8,128)}, ...), condition=%wide.region_9.10_spmd.clone, body=%wide.region_8.9_spmd.clone.sunk | while | flops 262148 | bytes 789609 | solution.py:47
  189.4 1.1 fusion.60
  190.5 1.1 fusion.60
  191.7 1.1 fusion.60
  192.9 1.1 fusion.60
  194.1 1.1 fusion.60
  195.3 1.1 fusion.60
  196.5 1.1 fusion.60
  197.7 1.1 fusion.60
  198.9 1.1 fusion.60
  200.1 1.1 fusion.60
  201.2 1.1 fusion.60
  202.4 1.1 fusion.60
  225.1 3.9 fusion.45
  229.0 117.8 %all-reduce.8.cloned.1.call-done = (f32[9,256,256]{2,1,0:T(8,128)}, f32[256,256]{0,1:T(8,128)}) async-done(((f32[9,256,256]{2,1,0:T(8,128)}, f32[256,256]{0,1:T(8,128)}), (f32[9,256,256]{2,1,0:T(8,128)}, f32[256,256]{0,1:T(8,128)})) %all-reduce.8.cloned.1.call-update) | async-done | bytes 2621456 | tf_op jit(solution)/shard_map/psum | solution.py:12
  346.9 3.5 collective-permute-start.2
  350.4 1.3 collective-permute-start.3
  352.3 4.3 collective-permute-done.3
  357.7 1.5 fusion.4
  359.2 76.2 %all-reduce.10.cloned.1.call-done = (f32[9,256,256]{2,1,0:T(8,128)}, f32[256,256]{0,1:T(8,128)}) async-done(((f32[9,256,256]{2,1,0:T(8,128)}, f32[256,256]{0,1:T(8,128)}), (f32[9,256,256]{2,1,0:T(8,128)}, f32[256,256]{0,1:T(8,128)})) %all-reduce.10.cloned.1.call-update) | async-done | bytes 2621456 | tf_op jit(solution)/shard_map/psum | solution.py:13
  435.5 1.7 dynamic-slice_multiply_fusion
  437.2 1.4 dynamic-slice_multiply_fusion.1
  (163 shorter events, 35.6 us)
Async XLA Ops:
  7.2 13.5 %copy-start = (bf16[9,256,256]{2,1,0:T(8,128)(2,1)S(1)}, bf16[9,256,256]{2,1,0:T(8,128)(2,1)}, u32[]{:S(2)}) copy-start(bf16[9,256,256]{2,1,0:T(8,128)(2,1)} %param.17) | copy-start | bytes 3538948
  7.2 13.2 %copy-start.1 = (bf16[2,4,64,256]{3,2,1,0:T(8,128)(2,1)S(1)}, bf16[2,4,64,256]{3,2,1,0:T(8,128)(2,1)}, u32[]{:S(2)}) copy-start(bf16[2,4,64,256]{3,2,1,0:T(8,128)(2,1)} %param.15) | copy-start | bytes 786436
  7.2 76.8 %all-gather.4.cloned.1.call-start = ((), (), s32[]{:S(2)}) async-start(), calls=%async_computation | async-start | bytes 8650752 | tf_op jit(solution)/shard_map/all_gather | solution.py:35
  8.2 6.8 %collective-permute-start = (bf16[2,1,64,256]{3,2,1,0:T(8,128)(2,1)S(1)}, bf16[2,1,64,256]{3,2,1,0:T(8,128)(2,1)S(1)}, u32[]{:S(2)}, u32[]{:S(2)}) collective-permute-start(bf16[2,1,64,256]{3,2,1,0:T(8,128)(2,1)S(1)} %get-tuple-element.438), channel_id=1, source_target_pairs={{0,1},{1,2},{2,3},{3,4},{4,5},{5,6},{6,7},{8,9},{9,10},{10,11},{11... | collective-permute-start | bytes 196616 | tf_op jit(solution)/shard_map/ppermute | solution.py:24
  12.1 6.2 %collective-permute-start.1 = (bf16[2,1,64,256]{3,2,1,0:T(8,128)(2,1)S(1)}, bf16[2,1,64,256]{3,2,1,0:T(8,128)(2,1)S(1)}, u32[]{:S(2)}, u32[]{:S(2)}) collective-permute-start(bf16[2,1,64,256]{3,2,1,0:T(8,128)(2,1)S(1)} %get-tuple-element.439), channel_id=1, source_target_pairs={{1,0},{2,1},{3,2},{4,3},{5,4},{6,5},{7,6},{9,8},{10,9},{11,10},{12... | collective-permute-start | bytes 196616 | tf_op jit(solution)/shard_map/ppermute | solution.py:26
  20.6 1.5 copy-start.2
  20.6 1.5 copy-start.4
  23.2 157.2 %all-gather.6.cloned.1.call-start = ((), (), s32[]{:S(2)}) async-start(), calls=%async_computation.1 | async-start | bytes 8650752 | tf_op jit(solution)/shard_map/all_gather | solution.py:35
  84.0 37.0 %copy-start.3 = (bf16[256,256]{1,0:T(8,128)(2,1)S(1)}, bf16[256,256]{1,0:T(8,128)(2,1)}, u32[]{:S(2)}) copy-start(bf16[256,256]{1,0:T(8,128)(2,1)} %param.18) | copy-start | bytes 393220
  84.0 37.0 %copy-start.5 = (bf16[2,4,64,256]{3,2,1,0:T(8,128)(2,1)S(1)}, bf16[2,4,64,256]{3,2,1,0:T(8,128)(2,1)}, u32[]{:S(2)}) copy-start(bf16[2,4,64,256]{3,2,1,0:T(8,128)(2,1)} %param.16) | copy-start | bytes 786436
  122.8 224.0 %all-reduce.8.cloned.1.call-start = ((), (), s32[]{:S(2)}) async-start(), calls=%async_computation.2 | async-start | bytes 5242880 | tf_op jit(solution)/shard_map/psum | solution.py:12
  229.0 206.5 %all-reduce.10.cloned.1.call-start = ((), (), s32[]{:S(2)}) async-start(), calls=%async_computation.3 | async-start | bytes 5242880 | tf_op jit(solution)/shard_map/psum | solution.py:13
  346.9 5.4 %collective-permute-start.2 = (bf16[2,1,64,256]{3,2,1,0:T(8,128)(2,1)S(1)}, bf16[2,1,64,256]{3,2,1,0:T(8,128)(2,1)S(1)}, u32[]{:S(2)}, u32[]{:S(2)}) collective-permute-start(bf16[2,1,64,256]{3,2,1,0:T(8,128)(2,1)S(1)} %get-tuple-element.436), channel_id=1, source_target_pairs={{0,1},{1,2},{2,3},{3,4},{4,5},{5,6},{6,7},{8,9},{9,10},{10,11},{11... | collective-permute-start | bytes 196616 | tf_op jit(solution)/shard_map/ppermute | solution.py:24
  350.4 6.2 %collective-permute-start.3 = (bf16[2,1,64,256]{3,2,1,0:T(8,128)(2,1)S(1)}, bf16[2,1,64,256]{3,2,1,0:T(8,128)(2,1)S(1)}, u32[]{:S(2)}, u32[]{:S(2)}) collective-permute-start(bf16[2,1,64,256]{3,2,1,0:T(8,128)(2,1)S(1)} %get-tuple-element.437), channel_id=1, source_target_pairs={{1,0},{2,1},{3,2},{4,3},{5,4},{6,5},{7,6},{9,8},{10,9},{11,10},{12... | collective-permute-start | bytes 196616 | tf_op jit(solution)/shard_map/ppermute | solution.py:26
  356.7 1.0 copy-start.6
  356.7 0.9 copy-start.7
Sparse Core Ops, SparseCore 0:
  23.3 60.6 all-gather.3
  123.0 57.4 all-gather.5
  229.1 117.7 all-reduce.7
  349.2 86.2 all-reduce.9
